TPU v7x, 32 devices: a whole 2x2x4 slice. The times are simulated.
32 devices in a mesh: seq: 2 (over x), head: 4 (over z), pool: 4 (over y, core).
Axes of the slice: x: 2, y: 2, z: 4, core: 2. Of those that a mesh axis runs over, the one named last changes fastest.
Arguments:
- tokens: bfloat16 [32, 4096], P(('seq', 'head'), 'pool'), may hold values from -6 to 6
- routes: int32 [32, 8], P(('seq', 'head')), may hold values from 0 to 15, all different within a row; in each aligned block of 4 rows (0 to 3, 4 to 7, ...) at most 2 rows name the same one
- gate_fixed: int32 [32, 8], P(('seq', 'head')), may hold values from 1 to 65535
- gate_weight: bfloat16 [16, 4096, 3072], P('seq', 'pool', 'head'), may hold values from -0.09375 to 0.09375
- up_weight: bfloat16 [16, 4096, 3072], P('seq', 'pool', 'head'), may hold values from -0.09375 to 0.09375
- down_weight: bfloat16 [16, 3072, 4096], P('seq', 'head', 'pool'), may hold values from -0.109375 to 0.109375
- gate_scale: bfloat16 [16, 32, 24], P('seq', 'pool', 'head'), may hold values from 0.5 to 2
- up_scale: bfloat16 [16, 32, 24], P('seq', 'pool', 'head'), may hold values from 0.5 to 2
- down_scale: bfloat16 [16, 24, 32], P('seq', 'head', 'pool'), may hold values from 0.5 to 2
Outputs:
- combined: bfloat16 [32, 4096], P(('seq', 'head'), 'pool')
Inputs may be any that keep to these rules, and one draw needn't show every extreme that they name: `routes`: each row names 8 different experts. Within the rows of one device (aligned blocks of 4 rows) no expert is named by more than 2 rows, and in some blocks one expert is named by exactly 2 rows.
All inputs are finite; a program needn't handle non-finite values.
Results may differ from a plain program's by a relative error of at most 0.02.
Values may be sent and summed in bfloat16 or wider, within the bound.
No kernel may reach another device: no remote copies, remote signals or barrier semaphores. Data moves between devices by JAX's collectives and lax.ppermute only.
A program may use at most 128 MiB of HBM per device.

v0:
```python
import jax
import jax.numpy as jnp
from jax import lax
from jax.sharding import PartitionSpec as P

QB = 128
CAP = 2
largest_choice = lax.Precision.HIGHEST


def expand_scale(route_weight, scale):
    grown = jnp.repeat(jnp.repeat(scale, QB, axis=1), QB, axis=2)
    return route_weight * grown


def slot_positions(block_routes, expert_total):
    flattened = block_routes.reshape(-1)
    expert_ids = lax.broadcasted_iota(jnp.int32, (1, expert_total), 1)
    onehot = (flattened[:, None] == expert_ids).astype(jnp.int32)
    before = jnp.cumsum(onehot, axis=0) - onehot
    slot_index = jnp.sum(before * onehot, axis=1)
    return (flattened * CAP + slot_index).reshape(block_routes.shape)


def local_buffer(tokens, positions, slot_total):
    targets = lax.broadcasted_iota(jnp.int32, (slot_total, 1, 1), 0)
    selector = jnp.any(positions[None, :, :] == targets, axis=2).astype(jnp.bfloat16)
    return jnp.dot(selector, tokens, preferred_element_type=jnp.float32).astype(jnp.bfloat16)


def per_device(
    tokens,
    routes,
    gate_fixed,
    gate_weight,
    up_weight,
    down_weight,
    gate_scale,
    up_scale,
    down_scale,
):
    seq_count = lax.axis_size("seq")
    head_count = lax.axis_size("head")
    local_experts = gate_weight.shape[0]
    expert_total = local_experts * seq_count
    feature_width = tokens.shape[1]
    slot_total = expert_total * CAP
    block_total = seq_count * head_count
    gate_dense = expand_scale(gate_weight, gate_scale)
    up_dense = expand_scale(up_weight, up_scale)
    down_dense = expand_scale(down_weight, down_scale)
    positions = slot_positions(routes, expert_total)
    outgoing = local_buffer(tokens, positions, slot_total)
    outgoing = outgoing.reshape(seq_count, 1, local_experts, 1, CAP, feature_width)
    outgoing = jnp.broadcast_to(
        outgoing, (seq_count, head_count, local_experts, 1, CAP, feature_width)
    )
    outgoing = outgoing.reshape(block_total, local_experts, 1, CAP, feature_width)
    arrived = lax.all_to_all(outgoing, ("seq", "head"), split_axis=0, concat_axis=2, tiled=True)
    slot_rows = arrived.reshape(local_experts, seq_count, head_count, CAP, feature_width)
    gate_sum = jnp.einsum(
        "jshcd,jdf->jshcf", slot_rows, gate_dense, preferred_element_type=jnp.float32
    )
    up_sum = jnp.einsum("jshcd,jdf->jshcf", slot_rows, up_dense, preferred_element_type=jnp.float32)
    gate_sum, up_sum = (
        lax.psum(gate_sum.astype(jnp.bfloat16), "pool").astype(jnp.float32),
        lax.psum(up_sum.astype(jnp.bfloat16), "pool").astype(jnp.float32),
    )
    hidden = (jax.nn.silu(gate_sum) * up_sum).astype(jnp.bfloat16)
    partial_out = jnp.einsum(
        "jshcf,jfd->jshcd", hidden, down_dense, preferred_element_type=jnp.float32
    )
    sending = partial_out.astype(jnp.bfloat16).reshape(
        local_experts, block_total, CAP, feature_width
    )
    gathered_back = lax.all_to_all(
        sending, ("seq", "head"), split_axis=1, concat_axis=0, tiled=True
    )
    gathered_back = gathered_back.reshape(seq_count, head_count, local_experts, CAP, feature_width)
    results = jnp.sum(gathered_back.astype(jnp.float32), axis=1).astype(jnp.bfloat16)
    results = results.reshape(slot_total, feature_width)
    fixed = gate_fixed.astype(jnp.float32)
    weights = fixed / jnp.sum(fixed, axis=1, keepdims=True)
    slot_ids = lax.broadcasted_iota(jnp.int32, (1, 1, slot_total), 2)
    combine_weight = jnp.sum(
        jnp.where(positions[:, :, None] == slot_ids, weights[:, :, None], 0.0), axis=1
    )
    combined = jnp.dot(
        combine_weight,
        results.astype(jnp.float32),
        precision=largest_choice,
        preferred_element_type=jnp.float32,
    )
    return combined.astype(jnp.bfloat16)


def solution(mesh):
    return jax.shard_map(
        per_device,
        mesh=mesh,
        in_specs=(
            P(("seq", "head"), "pool"),
            P(("seq", "head"), None),
            P(("seq", "head"), None),
            P("seq", "pool", "head"),
            P("seq", "pool", "head"),
            P("seq", "head", "pool"),
            P("seq", "pool", "head"),
            P("seq", "pool", "head"),
            P("seq", "head", "pool"),
        ),
        out_specs=P(("seq", "head"), "pool"),
        check_vma=False,
    )
```

profile of v0, /device:TPU:0, one launch (start us, length us, event | category | flops | bytes accessed | tf_op | source)
XLA Modules:
  0.0 150.8 jit_solution(4185804847729853960)
XLA Ops:
  6.5 0.8 eq.20
  7.4 0.2 select_reduce_fusion.1
  7.7 0.7 multiply_add_fusion
  8.5 0.2 convolution_convert_fusion
  8.8 0.7 broadcast_in_dim.44
  9.5 7.3 %all-to-all-start = ((bf16[8,8,1,2,1024]{4,1,3,2,0:T(8,128)(2,1)}), bf16[8,8,1,2,1024]{4,1,3,2,0:T(8,128)(2,1)S(1)}, u32[]{:S(2)}, u32[]{:S(2)}) async-start(bf16[8,8,1,2,1024]{4,1,3,2,0:T(8,128)(2,1)} %bitcast), calls=%async_computation | async-start | bytes 524288 | tf_op jit(solution)/shard_map/all_to_all | solution.py:59
  16.9 16.6 %copy.58 = bf16[8,1024,768]{1,2,0:T(8,128)(2,1)} copy(bf16[8,1024,768]{2,1,0:T(8,128)(2,1)} %param.12) | data formatting | bytes 25165824 | tf_op args[3]
  33.8 16.6 %copy.62 = bf16[8,1024,768]{1,2,0:T(8,128)(2,1)} copy(bf16[8,1024,768]{2,1,0:T(8,128)(2,1)} %param.13) | data formatting | bytes 25165824 | tf_op args[4]
  50.4 0.1 broadcast_in_dim.48
  50.6 11.1 %bitcast_multiply_fusion.1 = bf16[8,1024,768]{1,2,0:T(8,128)(2,1)} fusion(bf16[8,1024,768]{1,2,0:T(8,128)(2,1)} %copy.58, bf16[8,1024,6]{1,2,0:T(8,128)(2,1)S(1)} %copy.57), kind=kLoop, calls=%fused_computation.7 | loop fusion | flops 6291456 | bytes 25264128 | tf_op jit(solution)/shard_map/mul | solution.py:13
  61.8 1.8 %copy-done.3 = bf16[8,1024,768]{1,2,0:T(8,128)(2,1)S(1)} copy-done((bf16[8,1024,768]{1,2,0:T(8,128)(2,1)S(1)}, bf16[8,1024,768]{1,2,0:T(8,128)(2,1)}, u32[]{:S(2)}) %copy-start.3) | copy-done | bytes 12582936
  63.5 5.2 %bitcast_multiply_fusion = bf16[8,1024,768]{1,2,0:T(8,128)(2,1)} fusion(bf16[8,1024,768]{1,2,0:T(8,128)(2,1)S(1)} %copy-done.3, bf16[8,1024,6]{1,2,0:T(8,128)(2,1)S(1)} %copy.61), kind=kLoop, calls=%fused_computation.6 | loop fusion | flops 6291456 | bytes 25264128 | tf_op jit(solution)/shard_map/mul | solution.py:13
  68.8 8.9 %fusion.10 = bf16[8,2,4,2,768]{4,2,3,1,0:T(4,128)(2,1)} fusion(bf16[8,1024,768]{1,2,0:T(8,128)(2,1)} %bitcast_multiply_fusion.1, bf16[8,2,4,2,1024]{4,0,3,2,1:T(8,128)(2,1)S(1)} %bitcast.54), kind=kOutput, calls=%fused_computation.10 | convolution fusion | flops 201424896 | bytes 13041664 | tf_op jit(solution)/shard_map/jshcd,jdf->jshcf/dot_general | solution.py:61
  77.7 4.2 %fusion.13 = bf16[8,2,4,2,768]{4,2,3,1,0:T(4,128)(2,1)} fusion(bf16[8,1024,768]{1,2,0:T(8,128)(2,1)S(1)} %copy-done.2, bf16[8,2,4,2,1024]{4,0,3,2,1:T(8,128)(2,1)S(1)} %bitcast.55), kind=kOutput, calls=%fused_computation.11 | convolution fusion | flops 201424896 | bytes 13041664 | tf_op jit(solution)/shard_map/jshcd,jdf->jshcf/dot_general | solution.py:64
  81.9 0.2 broadcast_in_dim.50
  82.1 8.9 %broadcast_in_dim.51 = bf16[8,768,8,128]{3,2,1,0:T(8,128)(2,1)} broadcast(bf16[8,768,8]{2,1,0:T(8,128)(2,1)S(1)} %bitcast.53), dimensions={0,1,2} | broadcast | bytes 12681216 | tf_op jit(solution)/shard_map/broadcast_in_dim | solution.py:12
  91.0 19.4 %reshape.62 = bf16[8,768,1024]{2,1,0:T(8,128)(2,1)} reshape(bf16[8,768,8,128]{3,2,1,0:T(8,128)(2,1)} %broadcast_in_dim.51) | data formatting | bytes 25165824 | tf_op jit(solution)/shard_map/reshape | solution.py:12
  110.4 6.0 %all-reduce.3.cloned.1.call-done = (bf16[8,2,4,2,768]{4,2,3,1,0:T(4,128)(2,1)}, bf16[8,2,4,2,768]{4,2,3,1,0:T(4,128)(2,1)}) async-done(((bf16[8,2,4,2,768]{4,2,3,1,0:T(4,128)(2,1)}, bf16[8,2,4,2,768]{4,2,3,1,0:T(4,128)(2,1)}), (bf16[8,2,4,2,768]{4,2,3,1,0:T(4,128)(2,1)}, bf16[8,2,4,2,768]{4,2,3,1,0:T(4,128)(2,1)})) %all-reduce.3.cloned.1.call-update) | async-done | bytes 393232 | tf_op jit(solution)/shard_map/psum | solution.py:67
  116.4 11.4 %fusion.7 = bf16[8,2,4,2,1024]{4,2,3,1,0:T(4,128)(2,1)S(1)} fusion(bf16[8,768,1024]{2,1,0:T(8,128)(2,1)} %param.14, bf16[8,768,1024]{2,1,0:T(8,128)(2,1)} %reshape.62, bf16[8,2,4,2,768]{4,2,3,1,0:T(4,128)(2,1)} %get-tuple-element.5, bf16[8,2,4,2,768]{4,2,3,1,0:T(4,128)(2,1)} %get-tuple-element.6), kind=kOutput, calls=%fused_computation.9 | convolution fusion | flops 208535552 | bytes 25821184 | tf_op jit(solution)/shard_map/jshcf,jfd->jshcd/dot_general | solution.py:70
  127.8 0.8 copy.66
  128.6 5.5 %all-to-all-start.1 = ((bf16[8,8,2,1024]{3,0,2,1:T(8,128)(2,1)}), bf16[8,8,2,1024]{3,0,2,1:T(8,128)(2,1)S(1)}, u32[]{:S(2)}, u32[]{:S(2)}) async-start(bf16[8,8,2,1024]{3,0,2,1:T(8,128)(2,1)} %bitcast.13), calls=%async_computation.1 | async-start | bytes 524288 | tf_op jit(solution)/shard_map/all_to_all | solution.py:76
  134.1 0.1 convert_reduce_fusion
  134.4 8.6 %all-to-all-done.1 = bf16[8,8,2,1024]{3,0,2,1:T(8,128)(2,1)S(1)} async-done(((bf16[8,8,2,1024]{3,0,2,1:T(8,128)(2,1)}), bf16[8,8,2,1024]{3,0,2,1:T(8,128)(2,1)S(1)}, u32[]{:S(2)}, u32[]{:S(2)}) %all-to-all-start.1) | async-done | bytes 262176 | tf_op jit(solution)/shard_map/all_to_all | solution.py:76
  143.2 0.8 convolution_convert_fusion.1
  (35 shorter events, 1.1 us)
Async XLA Ops:
  6.5 2.0 %copy-start = (bf16[4,1024]{1,0:T(4,128)(2,1)S(1)}, bf16[4,1024]{1,0:T(4,128)(2,1)}, u32[]{:S(2)}) copy-start(bf16[4,1024]{1,0:T(4,128)(2,1)} %param.9) | copy-start | bytes 24580
  9.5 59.3 %all-to-all-start = ((bf16[8,8,1,2,1024]{4,1,3,2,0:T(8,128)(2,1)}), bf16[8,8,1,2,1024]{4,1,3,2,0:T(8,128)(2,1)S(1)}, u32[]{:S(2)}, u32[]{:S(2)}) async-start(bf16[8,8,1,2,1024]{4,1,3,2,0:T(8,128)(2,1)} %bitcast), calls=%async_computation | async-start | bytes 524288 | tf_op jit(solution)/shard_map/all_to_all | solution.py:59
  16.8 16.7 %copy-start.4 = (bf16[8,8,6]{1,0,2:T(8,128)(2,1)S(1)}, bf16[8,8,6]{1,0,2:T(8,128)(2,1)}, u32[]{:S(2)}) copy-start(bf16[8,8,6]{1,0,2:T(8,128)(2,1)} %param.15) | copy-start | bytes 2308
  16.8 99.6 %all-reduce.3.cloned.1.call-start = ((), (), s32[]{:S(2)}) async-start(), calls=%async_computation.2 | async-start | bytes 786432 | tf_op jit(solution)/shard_map/psum | solution.py:67
  33.7 16.6 %copy-start.5 = (bf16[8,8,6]{1,0,2:T(8,128)(2,1)S(1)}, bf16[8,8,6]{1,0,2:T(8,128)(2,1)}, u32[]{:S(2)}) copy-start(bf16[8,8,6]{1,0,2:T(8,128)(2,1)} %param.16) | copy-start | bytes 2308
  50.6 12.9 %copy-start.3 = (bf16[8,1024,768]{1,2,0:T(8,128)(2,1)S(1)}, bf16[8,1024,768]{1,2,0:T(8,128)(2,1)}, u32[]{:S(2)}) copy-start(bf16[8,1024,768]{1,2,0:T(8,128)(2,1)} %copy.62) | copy-start | bytes 37748740
  68.8 8.9 %copy-start.2 = (bf16[8,1024,768]{1,2,0:T(8,128)(2,1)S(1)}, bf16[8,1024,768]{1,2,0:T(8,128)(2,1)}, u32[]{:S(2)}) copy-start(bf16[8,1024,768]{1,2,0:T(8,128)(2,1)} %bitcast_multiply_fusion) | copy-start | bytes 37748740
  68.8 13.1 %copy-start.6 = (bf16[8,6,8]{2,0,1:T(8,128)(2,1)S(1)}, bf16[8,6,8]{2,0,1:T(8,128)(2,1)}, u32[]{:S(2)}) copy-start(bf16[8,6,8]{2,0,1:T(8,128)(2,1)} %param.17) | copy-start | bytes 2308
  116.4 27.5 %copy-start.1 = (bf16[4,1024]{1,0:T(4,128)(2,1)S(1)}, bf16[4,1024]{1,0:T(4,128)(2,1)}, u32[]{:S(2)}) copy-start(bf16[4,1024]{1,0:T(4,128)(2,1)} %param.9) | copy-start | bytes 24580
  116.4 17.8 %copy-start.7 = (s32[4,8]{1,0:T(4,128)S(1)}, s32[4,8]{1,0:T(4,128)}, u32[]{:S(2)}) copy-start(s32[4,8]{1,0:T(4,128)} %param.11) | copy-start | bytes 388
  128.6 14.4 %all-to-all-start.1 = ((bf16[8,8,2,1024]{3,0,2,1:T(8,128)(2,1)}), bf16[8,8,2,1024]{3,0,2,1:T(8,128)(2,1)S(1)}, u32[]{:S(2)}, u32[]{:S(2)}) async-start(bf16[8,8,2,1024]{3,0,2,1:T(8,128)(2,1)} %bitcast.13), calls=%async_computation.1 | async-start | bytes 524288 | tf_op jit(solution)/shard_map/all_to_all | solution.py:76
Sparse Core Ops, SparseCore 0:
  82.0 34.2 all-reduce.2
where the time goes:
time: 152 us; the launch traced here: 151 us
  local copies, waits for them, and re-layouts  66.6 us (44%)
  matrix products  25.5 us (17%)
  other arithmetic  17.8 us (12%)
  waiting for transfers between devices  14.6 us (10%)
  between operations  13.5 us (9%)
  starting transfers between devices  12.8 us (8%)
    unnamed x19, local copies, waits for them, and re-layouts  35.1 us
    reshape x5, local copies, waits for them, and re-layouts, expand_scale(): grown = jnp.repeat(jnp.repeat(scale, QB, axis=1), QB, axis=2)  19.6 us
    mul x2, other arithmetic, expand_scale(): return route_weight * grown  16.4 us
    dot_general x1, matrix products, per_device(): jnp.einsum('jshcf,jfd->jshcd', hidden, down_dense, preferred_element_type...  11.4 us
    broadcast_in_dim x4, local copies, waits for them, and re-layouts, expand_scale(): grown = jnp.repeat(jnp.repeat(scale, QB, axis=1), QB, axis=2)  9.3 us
    dot_general x1, matrix products, per_device(): jnp.einsum('jshcd,jdf->jshcf', slot_rows, gate_dense, preferred_element_t...  8.89 us
    all_to_all x1, waiting for transfers between devices, per_device(): lax.all_to_all(sending, ('seq', 'head'), split_axis=1, concat_axis=0, til...  8.59 us
    all_to_all x1, starting transfers between devices, per_device(): lax.all_to_all(outgoing, ('seq', 'head'), split_axis=0, concat_axis=2, ti...  7.28 us
  transfers between devices with their start and end apart: 3, of which 2 were waited for; matrix products, arithmetic and copies ran while one was open for 52% of the time, Pallas kernels for 0%

commit v1 on v0

--- a/solution.py
+++ b/solution.py
@@ -1,11 +1,25 @@
+import functools
 import jax
 import jax.numpy as jnp
 from jax import lax
 from jax.sharding import PartitionSpec as P
+from jax.lax import all_to_all, axis_size
 
 QB = 128
 CAP = 2
 largest_choice = lax.Precision.HIGHEST
+
+
+def mark_region_up(row_data, net_axis):
+    f_now = axis_size(net_axis)
+    v_next = jnp.split(row_data, f_now, axis=1)
+    later = jnp.stack(v_next, axis=0)
+    out_arr = all_to_all(later, net_axis, 0, 0)
+    carry = jnp.concatenate(out_arr, axis=0)
+    return carry
+
+
+_raise_edge = functools.partial(mark_region_up, net_axis=("seq", "head"))
 
 
 def expand_scale(route_weight, scale):
@@ -73,9 +87,7 @@
     sending = partial_out.astype(jnp.bfloat16).reshape(
         local_experts, block_total, CAP, feature_width
     )
-    gathered_back = lax.all_to_all(
-        sending, ("seq", "head"), split_axis=1, concat_axis=0, tiled=True
-    )
+    gathered_back = _raise_edge(sending)
     gathered_back = gathered_back.reshape(seq_count, head_count, local_experts, CAP, feature_width)
     results = jnp.sum(gathered_back.astype(jnp.float32), axis=1).astype(jnp.bfloat16)
     results = results.reshape(slot_total, feature_width)

time: 152 us -> 157 us (1.033)
  local copies, waits for them, and re-layouts: 66.6 us -> 70.7 us
    unnamed x19 -> x26, local copies, waits for them, and re-layouts: 35.1 us -> 39.3 us
  transfers between devices with their start and end apart: 3 -> 3, of which waited for: 2 -> 2; matrix products, arithmetic and copies ran while one was open for 52% -> 51% of each run, Pallas kernels for 0% -> 0%
where the time goes in v1:
time: 157 us; the launch traced here: 155 us
  local copies, waits for them, and re-layouts  70.7 us (45%)
  matrix products  25.5 us (16%)
  other arithmetic  17.8 us (11%)
  waiting for transfers between devices  14.6 us (9%)
  between operations  13.6 us (9%)
  starting transfers between devices  12.8 us (8%)
    unnamed x26, local copies, waits for them, and re-layouts  39.3 us
    reshape x5, local copies, waits for them, and re-layouts, expand_scale(): grown = jnp.repeat(jnp.repeat(scale, QB, axis=1), QB, axis=2)  19.6 us
    mul x2, other arithmetic, expand_scale(): return route_weight * grown  16.4 us
    dot_general x1, matrix products, per_device(): jnp.einsum('jshcf,jfd->jshcd', hidden, down_dense, preferred_element_type...  11.4 us
    broadcast_in_dim x4, local copies, waits for them, and re-layouts, expand_scale(): grown = jnp.repeat(jnp.repeat(scale, QB, axis=1), QB, axis=2)  9.3 us
    dot_general x1, matrix products, per_device(): jnp.einsum('jshcd,jdf->jshcf', slot_rows, gate_dense, preferred_element_t...  8.89 us
    all_to_all x1, waiting for transfers between devices, mark_region_up(): out_arr = all_to_all(later, net_axis, 0, 0)  8.59 us
    all_to_all x1, starting transfers between devices, per_device(): lax.all_to_all(outgoing, ('seq', 'head'), split_axis=0, concat_axis=2, ti...  7.28 us
  transfers between devices with their start and end apart: 3, of which 2 were waited for; matrix products, arithmetic and copies ran while one was open for 51% of the time, Pallas kernels for 0%

profile of v1, /device:TPU:0, one launch (start us, length us, event | category | flops | bytes accessed | tf_op | source)
XLA Modules:
  0.0 154.9 jit_solution(7704751971942306038)
XLA Ops:
  6.5 0.8 eq.20
  7.7 0.7 multiply_add_fusion
  8.8 0.7 broadcast_in_dim.44
  9.5 7.3 %all-to-all-start = ((bf16[8,8,1,2,1024]{4,1,3,2,0:T(8,128)(2,1)}), bf16[8,8,1,2,1024]{4,1,3,2,0:T(8,128)(2,1)S(1)}, u32[]{:S(2)}, u32[]{:S(2)}) async-start(bf16[8,8,1,2,1024]{4,1,3,2,0:T(8,128)(2,1)} %bitcast), calls=%async_computation | async-start | bytes 524288 | tf_op jit(solution)/shard_map/all_to_all | solution.py:73
  16.9 16.6 %copy.65 = bf16[8,1024,768]{1,2,0:T(8,128)(2,1)} copy(bf16[8,1024,768]{2,1,0:T(8,128)(2,1)} %param.12) | data formatting | bytes 25165824 | tf_op args[3]
  33.8 16.6 %copy.69 = bf16[8,1024,768]{1,2,0:T(8,128)(2,1)} copy(bf16[8,1024,768]{2,1,0:T(8,128)(2,1)} %param.13) | data formatting | bytes 25165824 | tf_op args[4]
  50.6 11.1 %bitcast_multiply_fusion.1 = bf16[8,1024,768]{1,2,0:T(8,128)(2,1)} fusion(bf16[8,1024,768]{1,2,0:T(8,128)(2,1)} %copy.65, bf16[8,1024,6]{1,2,0:T(8,128)(2,1)S(1)} %copy.64), kind=kLoop, calls=%fused_computation.7 | loop fusion | flops 6291456 | bytes 25264128 | tf_op jit(solution)/shard_map/mul | solution.py:27
  61.8 1.8 %copy-done.3 = bf16[8,1024,768]{1,2,0:T(8,128)(2,1)S(1)} copy-done((bf16[8,1024,768]{1,2,0:T(8,128)(2,1)S(1)}, bf16[8,1024,768]{1,2,0:T(8,128)(2,1)}, u32[]{:S(2)}) %copy-start.3) | copy-done | bytes 12582936
  63.5 5.2 %bitcast_multiply_fusion = bf16[8,1024,768]{1,2,0:T(8,128)(2,1)} fusion(bf16[8,1024,768]{1,2,0:T(8,128)(2,1)S(1)} %copy-done.3, bf16[8,1024,6]{1,2,0:T(8,128)(2,1)S(1)} %copy.68), kind=kLoop, calls=%fused_computation.6 | loop fusion | flops 6291456 | bytes 25264128 | tf_op jit(solution)/shard_map/mul | solution.py:27
  68.8 8.9 %fusion.10 = bf16[8,2,4,2,768]{4,2,3,1,0:T(4,128)(2,1)} fusion(bf16[8,1024,768]{1,2,0:T(8,128)(2,1)} %bitcast_multiply_fusion.1, bf16[8,2,4,2,1024]{4,0,3,2,1:T(8,128)(2,1)S(1)} %bitcast.81), kind=kOutput, calls=%fused_computation.10 | convolution fusion | flops 201424896 | bytes 13041664 | tf_op jit(solution)/shard_map/jshcd,jdf->jshcf/dot_general | solution.py:75
  77.7 4.2 %fusion.13 = bf16[8,2,4,2,768]{4,2,3,1,0:T(4,128)(2,1)} fusion(bf16[8,1024,768]{1,2,0:T(8,128)(2,1)S(1)} %copy-done.2, bf16[8,2,4,2,1024]{4,0,3,2,1:T(8,128)(2,1)S(1)} %bitcast.82), kind=kOutput, calls=%fused_computation.11 | convolution fusion | flops 201424896 | bytes 13041664 | tf_op jit(solution)/shard_map/jshcd,jdf->jshcf/dot_general | solution.py:78
  82.1 8.9 %broadcast_in_dim.51 = bf16[8,768,8,128]{3,2,1,0:T(8,128)(2,1)} broadcast(bf16[8,768,8]{2,1,0:T(8,128)(2,1)S(1)} %bitcast.80), dimensions={0,1,2} | broadcast | bytes 12681216 | tf_op jit(solution)/shard_map/broadcast_in_dim | solution.py:26
  91.0 19.4 %reshape.58 = bf16[8,768,1024]{2,1,0:T(8,128)(2,1)} reshape(bf16[8,768,8,128]{3,2,1,0:T(8,128)(2,1)} %broadcast_in_dim.51) | data formatting | bytes 25165824 | tf_op jit(solution)/shard_map/reshape | solution.py:26
  110.4 6.0 %all-reduce.3.cloned.1.call-done = (bf16[8,2,4,2,768]{4,2,3,1,0:T(4,128)(2,1)}, bf16[8,2,4,2,768]{4,2,3,1,0:T(4,128)(2,1)}) async-done(((bf16[8,2,4,2,768]{4,2,3,1,0:T(4,128)(2,1)}, bf16[8,2,4,2,768]{4,2,3,1,0:T(4,128)(2,1)}), (bf16[8,2,4,2,768]{4,2,3,1,0:T(4,128)(2,1)}, bf16[8,2,4,2,768]{4,2,3,1,0:T(4,128)(2,1)})) %all-reduce.3.cloned.1.call-update) | async-done | bytes 393232 | tf_op jit(solution)/shard_map/psum | solution.py:81
  116.4 11.4 %fusion.7 = bf16[8,2,4,2,1024]{4,2,3,1,0:T(4,128)(2,1)S(1)} fusion(bf16[8,768,1024]{2,1,0:T(8,128)(2,1)} %param.14, bf16[8,768,1024]{2,1,0:T(8,128)(2,1)} %reshape.58, bf16[8,2,4,2,768]{4,2,3,1,0:T(4,128)(2,1)} %get-tuple-element.5, bf16[8,2,4,2,768]{4,2,3,1,0:T(4,128)(2,1)} %get-tuple-element.6), kind=kOutput, calls=%fused_computation.9 | convolution fusion | flops 208535552 | bytes 25821184 | tf_op jit(solution)/shard_map/jshcf,jfd->jshcd/dot_general | solution.py:84
  127.9 0.6 fusion.31
  128.5 0.6 fusion.30
  129.7 0.6 fusion.28
  131.0 0.6 fusion.26
  131.6 0.6 fusion.25
  132.2 0.6 fusion.24
  132.8 5.5 %all-to-all-start.1 = ((bf16[8,8,1,2,1024]{4,1,3,2,0:T(8,128)(2,1)}), bf16[8,8,1,2,1024]{4,1,3,2,0:T(8,128)(2,1)S(1)}, u32[]{:S(2)}, u32[]{:S(2)}) async-start(bf16[8,8,1,2,1024]{4,1,3,2,0:T(8,128)(2,1)} %fusion.24), calls=%async_computation.1 | async-start | bytes 524288 | tf_op jit(solution)/shard_map/all_to_all | solution.py:17
  138.6 8.6 %all-to-all-done.1 = bf16[8,8,1,2,1024]{4,1,3,2,0:T(8,128)(2,1)S(1)} async-done(((bf16[8,8,1,2,1024]{4,1,3,2,0:T(8,128)(2,1)}), bf16[8,8,1,2,1024]{4,1,3,2,0:T(8,128)(2,1)S(1)}, u32[]{:S(2)}, u32[]{:S(2)}) %all-to-all-start.1) | async-done | bytes 262176 | tf_op jit(solution)/shard_map/all_to_all | solution.py:17
  147.3 0.8 convolution_convert_fusion.1
  (43 shorter events, 3.3 us)
Async XLA Ops:
  6.5 2.0 %copy-start = (bf16[4,1024]{1,0:T(4,128)(2,1)S(1)}, bf16[4,1024]{1,0:T(4,128)(2,1)}, u32[]{:S(2)}) copy-start(bf16[4,1024]{1,0:T(4,128)(2,1)} %param.9) | copy-start | bytes 24580
  9.5 59.3 %all-to-all-start = ((bf16[8,8,1,2,1024]{4,1,3,2,0:T(8,128)(2,1)}), bf16[8,8,1,2,1024]{4,1,3,2,0:T(8,128)(2,1)S(1)}, u32[]{:S(2)}, u32[]{:S(2)}) async-start(bf16[8,8,1,2,1024]{4,1,3,2,0:T(8,128)(2,1)} %bitcast), calls=%async_computation | async-start | bytes 524288 | tf_op jit(solution)/shard_map/all_to_all | solution.py:73
  16.8 16.7 %copy-start.4 = (bf16[8,8,6]{1,0,2:T(8,128)(2,1)S(1)}, bf16[8,8,6]{1,0,2:T(8,128)(2,1)}, u32[]{:S(2)}) copy-start(bf16[8,8,6]{1,0,2:T(8,128)(2,1)} %param.15) | copy-start | bytes 2308
  16.8 99.6 %all-reduce.3.cloned.1.call-start = ((), (), s32[]{:S(2)}) async-start(), calls=%async_computation.2 | async-start | bytes 786432 | tf_op jit(solution)/shard_map/psum | solution.py:81
  33.7 16.6 %copy-start.5 = (bf16[8,8,6]{1,0,2:T(8,128)(2,1)S(1)}, bf16[8,8,6]{1,0,2:T(8,128)(2,1)}, u32[]{:S(2)}) copy-start(bf16[8,8,6]{1,0,2:T(8,128)(2,1)} %param.16) | copy-start | bytes 2308
  50.6 12.9 %copy-start.3 = (bf16[8,1024,768]{1,2,0:T(8,128)(2,1)S(1)}, bf16[8,1024,768]{1,2,0:T(8,128)(2,1)}, u32[]{:S(2)}) copy-start(bf16[8,1024,768]{1,2,0:T(8,128)(2,1)} %copy.69) | copy-start | bytes 37748740
  68.8 8.9 %copy-start.2 = (bf16[8,1024,768]{1,2,0:T(8,128)(2,1)S(1)}, bf16[8,1024,768]{1,2,0:T(8,128)(2,1)}, u32[]{:S(2)}) copy-start(bf16[8,1024,768]{1,2,0:T(8,128)(2,1)} %bitcast_multiply_fusion) | copy-start | bytes 37748740
  68.8 13.1 %copy-start.6 = (bf16[8,6,8]{2,0,1:T(8,128)(2,1)S(1)}, bf16[8,6,8]{2,0,1:T(8,128)(2,1)}, u32[]{:S(2)}) copy-start(bf16[8,6,8]{2,0,1:T(8,128)(2,1)} %param.17) | copy-start | bytes 2308
  116.4 31.7 %copy-start.1 = (bf16[4,1024]{1,0:T(4,128)(2,1)S(1)}, bf16[4,1024]{1,0:T(4,128)(2,1)}, u32[]{:S(2)}) copy-start(bf16[4,1024]{1,0:T(4,128)(2,1)} %param.9) | copy-start | bytes 24580
  116.4 21.9 %copy-start.7 = (s32[4,8]{1,0:T(4,128)S(1)}, s32[4,8]{1,0:T(4,128)}, u32[]{:S(2)}) copy-start(s32[4,8]{1,0:T(4,128)} %param.11) | copy-start | bytes 388
  132.8 14.4 %all-to-all-start.1 = ((bf16[8,8,1,2,1024]{4,1,3,2,0:T(8,128)(2,1)}), bf16[8,8,1,2,1024]{4,1,3,2,0:T(8,128)(2,1)S(1)}, u32[]{:S(2)}, u32[]{:S(2)}) async-start(bf16[8,8,1,2,1024]{4,1,3,2,0:T(8,128)(2,1)} %fusion.24), calls=%async_computation.1 | async-start | bytes 524288 | tf_op jit(solution)/shard_map/all_to_all | solution.py:17
Sparse Core Ops, SparseCore 0:
  82.0 34.2 all-reduce.2
